TPU v7x, 128 devices: a whole 4x4x4 slice. The times are simulated.
128 devices in a mesh: tile: 32 (over x, y_hi, z), tm: 4 (over y_lo, core).
Axes of the slice: x: 4, y: 4 (y_hi: 2, y_lo: 2; y = y_hi * 2 + y_lo), z: 4, core: 2. Of those that a mesh axis runs over, the one named last changes fastest.
Arguments:
- volume: bfloat16 [16, 256, 16, 128], P('tm', 'tile'), may hold values from -6 to 6
- frame_index: int32 [16], P('tm'), may hold values from 0 to 31, as said below
- tile_offset: int32 [3], replicated, may hold values from 0 to 255
- conv_first: bfloat16 [16, 1, 3, 3, 3], replicated, may hold values from -1.25 to 1.25
- conv_second: bfloat16 [16, 16, 3, 3, 3], replicated, may hold values from -0.3125 to 0.3125
- patch_weight: bfloat16 [8192, 1024], replicated, may hold values from -0.5 to 0.5
- attend_weight: bfloat16 [1024, 3072], P(None, 'tile')
- mixing_weight: bfloat16 [1024, 1024], P(None, 'tile'), may hold values from -0.1875 to 0.1875
- cube_output_projector: bfloat16 [1024, 512], replicated, may hold values from -0.1875 to 0.1875
Outputs:
- prediction_tensor: bfloat16 [16, 32, 2, 16, 512], P('tm', 'tile')
Inputs may be any that keep to these rules, and one draw needn't show every extreme that they name: `frame_index`: strictly increasing; the first frame is 0 and the last is 31.
All inputs are finite; a program needn't handle non-finite values.
Results may differ from a plain program's by a relative error of at most 0.015.
Values may be sent and summed in bfloat16 or wider, within the bound.
No kernel may reach another device: no remote copies, remote signals or barrier semaphores. Data moves between devices by JAX's collectives and lax.ppermute only.
A program may use at most 256 MiB of HBM per device.

v0:
```python
import math
import jax
import jax.numpy as jnp
from jax import lax
from jax.sharding import PartitionSpec as P

CH = 16
D = 1024
HEADS = 8
HD = 128
BLOCK_EDGE_UNITS = 8


def with_halo(cells, sides, width):
    for axis, dim in sides:
        count = lax.axis_size(axis)
        ends = count - 1
        head = lax.slice_in_dim(cells, 0, width, axis=dim)
        tail = lax.slice_in_dim(cells, cells.shape[dim] - width, cells.shape[dim], axis=dim)
        cells = jnp.concatenate(
            [
                lax.ppermute(tail, axis, [(i, (i + 1) % count) for i in range(ends)]),
                cells,
                lax.ppermute(head, axis, [((i + 1) % count, i) for i in range(ends)]),
            ],
            axis=dim,
        )
    return cells


def convolve_strip(field_in, kernel):
    return lax.conv_general_dilated(
        field_in,
        kernel,
        (1, 1, 1),
        ((0, 0), (1, 1), (1, 1)),
        dimension_numbers=("NCDHW", "OIDHW", "NCDHW"),
        preferred_element_type=jnp.float32,
    )


def settle(values_in):
    return values_in * lax.rsqrt(jnp.mean(values_in * values_in, axis=-1, keepdims=True) + 1e-05)


def embed_time(frame_index):
    frequency = jnp.exp(-math.log(1000.0) * jnp.arange(D, dtype=jnp.float32) / D)
    phase_shift = (jnp.arange(D) % 2).astype(jnp.float32) * (math.pi / 2)
    return (jnp.sin(frame_index.astype(jnp.float32)[:, None] * frequency + phase_shift), frequency)


def embed_space(tile_offset, place_x, place_z, place_y, frequency):
    along_x = (tile_offset[0] + BLOCK_EDGE_UNITS * place_x).astype(jnp.float32)
    along_z = (tile_offset[1] + BLOCK_EDGE_UNITS * place_z).astype(jnp.float32)
    along_y = (tile_offset[2] + BLOCK_EDGE_UNITS * place_y).astype(jnp.float32)
    summed = jnp.sin(along_x[:, None, None, None] * frequency) + jnp.sin(
        along_z[None, :, None, None] * frequency + 1.0
    )
    summed = summed + jnp.sin(along_y[None, None, :, None] * frequency + 2.0)
    return summed.reshape(-1, D)


def attend_frames(query, keys_all, values_all, first_frame):
    cube_count = keys_all.shape[1]
    scores = jnp.einsum(
        "tnhd,smhd->htnsm", query, keys_all, preferred_element_type=jnp.float32
    ) / math.sqrt(HD)
    scores = scores.reshape(scores.shape[0], query.shape[0], query.shape[1], -1)
    query_frame = first_frame + jnp.arange(query.shape[0])
    allowed = jnp.arange(keys_all.shape[0])[None, :] <= query_frame[:, None]
    allowed = jnp.repeat(allowed, cube_count, axis=1)
    scores = jnp.where(allowed[None, :, None, :], scores, -1e30)
    shifted = jnp.exp(scores - jnp.max(scores, axis=-1, keepdims=True))
    weights = (shifted / jnp.sum(shifted, axis=-1, keepdims=True)).astype(jnp.bfloat16)
    flat_values = values_all.reshape(-1, values_all.shape[2], values_all.shape[3])
    return jnp.einsum(
        "htnk,khd->tnhd", weights, flat_values, preferred_element_type=jnp.float32
    ).astype(jnp.bfloat16)


def local(
    volume,
    frame_index,
    tile_offset,
    conv_first,
    conv_second,
    patch_weight,
    attend_weight,
    mixing_weight,
    cube_output_projector,
):
    local_frames, width_here, cells_in_depth, height_extent = volume.shape
    tile_place = lax.axis_index("tile")
    padded = with_halo(volume, (("tile", 1),), 1)
    first_maps = jax.nn.silu(convolve_strip(padded[:, None], conv_first)).astype(jnp.bfloat16)
    first_maps = with_halo(first_maps, (("tile", 2),), 1)
    second_maps = jax.nn.silu(convolve_strip(first_maps, conv_second)).astype(jnp.bfloat16)
    stride_along_x = width_here // BLOCK_EDGE_UNITS
    patch_cubes = second_maps.reshape(
        local_frames,
        CH,
        stride_along_x,
        BLOCK_EDGE_UNITS,
        cells_in_depth // BLOCK_EDGE_UNITS,
        BLOCK_EDGE_UNITS,
        height_extent // BLOCK_EDGE_UNITS,
        BLOCK_EDGE_UNITS,
    )
    patch_cubes = patch_cubes.transpose(0, 2, 4, 6, 1, 3, 5, 7).reshape(
        -1, CH * BLOCK_EDGE_UNITS**3
    )
    encoded = jnp.dot(patch_cubes, patch_weight, preferred_element_type=jnp.float32).reshape(
        local_frames, -1, D
    )
    time_emb, frequency = embed_time(frame_index)
    place_x = tile_place * stride_along_x + jnp.arange(stride_along_x)
    space_emb = embed_space(
        tile_offset,
        place_x,
        jnp.arange(cells_in_depth // BLOCK_EDGE_UNITS),
        jnp.arange(height_extent // BLOCK_EDGE_UNITS),
        frequency,
    )
    tokens = (encoded + time_emb[:, None, :] + space_emb[None]).astype(jnp.bfloat16)
    token_rows = tokens.reshape(-1, D)
    normed = settle(token_rows.astype(jnp.float32)).astype(jnp.bfloat16)
    row_count = token_rows.shape[0]
    projected = jnp.dot(
        normed,
        lax.all_gather(attend_weight, "tile", axis=1, tiled=True),
        preferred_element_type=jnp.float32,
    ).astype(jnp.bfloat16)
    cube_count = row_count // local_frames
    projected = projected.reshape(local_frames, cube_count, 3, HEADS, HD)
    keys_values = lax.all_gather(projected[:, :, 1:], "tm", axis=0, tiled=True)
    attended = attend_frames(
        projected[:, :, 0],
        keys_values[:, :, 0],
        keys_values[:, :, 1],
        lax.axis_index("tm") * local_frames,
    )
    attended_rows = attended.reshape(row_count, D)
    mixed_terms = jnp.dot(
        attended_rows,
        lax.all_gather(mixing_weight, "tile", axis=1, tiled=True),
        preferred_element_type=jnp.float32,
    )
    residual = token_rows.astype(jnp.float32) + mixed_terms
    ending_entries = settle(residual).astype(jnp.bfloat16)
    prediction_tensor = jnp.dot(
        ending_entries, cube_output_projector, preferred_element_type=jnp.float32
    ).astype(jnp.bfloat16)
    return prediction_tensor.reshape(
        local_frames,
        stride_along_x,
        cells_in_depth // BLOCK_EDGE_UNITS,
        height_extent // BLOCK_EDGE_UNITS,
        -1,
    )


def solution(mesh):
    placed = (
        P("tm", "tile", None, None),
        P("tm"),
        P(),
        P(),
        P(),
        P(),
        P(None, "tile"),
        P(None, "tile"),
        P(),
    )
    return jax.shard_map(
        local,
        mesh=mesh,
        in_specs=placed,
        out_specs=P("tm", "tile", None, None, None),
        check_vma=False,
    )
```

profile of v0, /device:TPU:0, one launch (start us, length us, event | category | flops | bytes accessed | tf_op | source)
XLA Modules:
  0.0 538.9 jit_solution(4593768674398260444)
XLA Ops:
  6.5 0.8 fusion.34
  7.4 3.9 collective-permute-start
  11.3 1.3 collective-permute-start.1
  12.7 1.4 fusion.35
  14.8 0.7 add_convert_fusion.1
  15.5 0.7 add_convert_fusion
  16.2 0.7 convert_element_type.69
  16.9 0.3 add_sine_fusion
  17.2 0.2 sine_add_fusion
  17.4 0.7 broadcast_add_fusion
  18.0 0.8 add_sine_fusion.1
  18.8 0.9 maximum_bitcast_fusion.1
  19.8 0.2 pad
  19.9 0.9 reshape.256
  20.9 0.4 slice.52
  21.3 0.2 copy.60
  21.5 2.0 fusion.6
  23.5 4.4 copy.19
  27.9 19.7 %multiply_convert_fusion.1 = bf16[8,16,32,17,16]{2,4,3,1,0:T(8,128)(2,1)} fusion(pred[32,17]{0,1:T(8,128)(4,1)S(1)} %copy-done.7, bf16[1,10,16,32,19]{3,0,4,2,1:T(2,128)(2,1)S(1)} %copy.19, bf16[16,1,3,3,3]{0,4,3,2,1:T(4,128)(2,1)S(1)} %copy-done.6), kind=kOutput, calls=%fused_computation.5 | convolution fusion | flops 64339968 | bytes 2424192 | tf_op jit(solution)/shard_map/conv_general_dilated | solution.py:32
  47.7 24.2 %copy.22 = bf16[8,16,32,17,16]{3,2,4,1,0:T(8,128)(2,1)} copy(bf16[8,16,32,17,16]{2,4,3,1,0:T(8,128)(2,1)} %multiply_convert_fusion.1) | data formatting | bytes 4456448 | tf_op jit(solution)/shard_map/convert_element_type | solution.py:95
  71.8 3.6 fusion.33
  75.4 3.6 copy.21
  79.0 2.3 reshape.260
  81.3 1.8 slice_bitcast_fusion.5
  83.1 4.3 collective-permute-start.2
  87.4 3.6 copy.23
  91.0 2.3 reshape.262
  93.3 1.1 slice_bitcast_fusion.4
  94.4 1.3 collective-permute-start.3
  95.7 21.7 %reshape.271 = bf16[8,16,4,136,16]{3,2,4,1,0:T(4,128)(2,1)} reshape(bf16[8,16,32,17,16]{3,2,4,1,0:T(8,128)(2,1)} %copy.22) | data formatting | bytes 4456448 | tf_op jit(solution)/shard_map/convert_element_type | solution.py:95
  117.4 2.6 slice_bitcast_fusion.1
  120.0 2.0 maximum_bitcast_fusion
  122.0 3.0 copy.42
  125.0 4.4 pad.2.clone
  129.4 24.7 %reshape.265 = bf16[16,10,16,4,8,17]{5,4,2,3,1,0:T(8,128)(2,1)} reshape(bf16[16,10,16,4,136]{4,2,3,1,0:T(8,128)(2,1)} %pad.2.clone) | data formatting | bytes 5570560 | tf_op jit(solution)/shard_map/conv_general_dilated | solution.py:32
  154.1 21.6 %slice.58 = bf16[16,10,16,4,7,2]{5,4,2,3,1,0:T(8,128)(2,1)} slice(bf16[16,10,16,4,8,17]{5,4,2,3,1,0:T(8,128)(2,1)} %reshape.265), slice={[0:16], [0:10], [0:16], [0:4], [1:8], [0:2]} | slice | bytes 573440 | tf_op jit(solution)/shard_map/conv_general_dilated | solution.py:32
  175.7 21.9 %copy_bitcast_fusion = bf16[16,10,16,32,19]{4,3,2,1,0:T(8,128)(2,1)} fusion(bf16[16,10,16,4,7,2]{5,4,2,3,1,0:T(8,128)(2,1)} %slice.58, bf16[16,10,16,4,8,17]{5,4,2,3,1,0:T(8,128)(2,1)S(1)} %copy-done.1), kind=kLoop, calls=%fused_computation.3 | loop fusion | flops 9338880 | bytes 6184960 | tf_op jit(solution)/shard_map/conv_general_dilated | solution.py:32
  197.7 28.3 %copy.26 = bf16[16,10,16,32,19]{3,0,4,2,1:T(8,128)(2,1)} copy(bf16[16,10,16,32,19]{4,3,2,1,0:T(8,128)(2,1)} %copy_bitcast_fusion) | data formatting | bytes 6225920 | tf_op jit(solution)/shard_map/conv_general_dilated | solution.py:32
  225.9 35.9 %multiply_convert_fusion = bf16[8,16,32,17,16]{2,4,3,1,0:T(8,128)(2,1)} fusion(bf16[16,10,16,32,19]{3,0,4,2,1:T(8,128)(2,1)} %copy.26, bf16[16,16,3,3,3]{1,0,4,3,2:T(8,128)(2,1)S(1)} %copy-done.5, pred[32,17]{0,1:T(8,128)(4,1)S(1)} %copy-done.7), kind=kOutput, calls=%fused_computation.4 | convolution fusion | flops 929169408 | bytes 5355552 | tf_op jit(solution)/shard_map/conv_general_dilated | solution.py:32
  261.9 24.1 %copy.27 = bf16[8,16,32,17,16]{3,2,4,1,0:T(8,128)(2,1)} copy(bf16[8,16,32,17,16]{2,4,3,1,0:T(8,128)(2,1)} %multiply_convert_fusion) | data formatting | bytes 4456448 | tf_op jit(solution)/shard_map/convert_element_type | solution.py:97
  286.0 21.3 %reshape.269 = bf16[8,16,4,136,16]{3,2,4,1,0:T(4,128)(2,1)} reshape(bf16[8,16,32,17,16]{3,2,4,1,0:T(8,128)(2,1)} %copy.27) | data formatting | bytes 4456448 | tf_op jit(solution)/shard_map/convert_element_type | solution.py:97
  307.3 2.6 slice_bitcast_fusion
  309.9 11.0 %copy.28 = bf16[4,16,8,16,128]{1,4,3,2,0:T(8,128)(2,1)} copy(bf16[4,16,8,16,128]{4,0,1,3,2:T(4,128)(2,1)S(1)} %slice_bitcast_fusion) | data formatting | bytes 4194304 | tf_op jit(solution)/shard_map/convert_element_type | solution.py:97
  320.9 51.2 %copy.29 = bf16[4,1,2,16,16,8,8,8]{3,2,7,6,5,4,0,1:T(2,128)(2,1)} copy(bf16[4,1,2,16,16,8,8,8]{4,7,3,6,2,5,0,1:T(8,128)(2,1)} %bitcast.117) | data formatting | bytes 4194304 | tf_op jit(solution)/shard_map/transpose | solution.py:109
  372.2 27.0 %dot_general.20 = bf16[4,32,8192]{1,2,0:T(8,128)(2,1)} reshape(bf16[4,1,2,16,16,8,8,8]{3,2,7,6,5,4,0,1:T(2,128)(2,1)} %copy.29) | data formatting | bytes 4194304 | tf_op jit(solution)/shard_map/dot_general | solution.py:112
  399.2 11.8 %multiply_reduce_fusion.1 = (f32[4,32]{1,0:T(4,128)S(1)}, f32[4,32,1024]{2,1,0:T(8,128)S(1)}) fusion(f32[32,1024]{1,0:T(8,128)S(1)} %bitcast.123, f32[4,1024]{1,0:T(4,128)S(1)} %copy-done.4, bf16[4,32,8192]{1,2,0:T(8,128)(2,1)} %dot_general.20, bf16[8192,1024]{1,0:T(8,128)(2,1)} %param.14), kind=kOutput, calls=%fused_computation.35 | convolution fusion | flops 2148270080 | bytes 19546624 | tf_op jit(solution)/shard_map/dot_general | solution.py:112
  411.0 0.1 rsqrt.20
  411.1 0.1 fusion.22
  411.2 5.0 fusion.7
  416.2 0.2 copy.43
  416.4 0.9 copy.40
  417.4 0.7 all-gather.8.cloned.1.call-update
  418.2 0.1 iota_compare_fusion.2
  418.2 0.1 broadcast_in_dim.23
  418.3 0.1 broadcast_in_dim.24
  418.5 35.0 %all-gather.6.cloned.1.call-done = bf16[16,32,2,8,128]{4,1,0,3,2:T(8,128)(2,1)} async-done(((bf16[4,32,2,8,128]{4,1,0,3,2:T(8,128)(2,1)}), bf16[16,32,2,8,128]{4,1,0,3,2:T(8,128)(2,1)}) %all-gather.6.cloned.1.call-update) | async-done | bytes 2097168 | tf_op jit(solution)/shard_map/all_gather | solution.py:135
  453.5 6.2 %select_reduce_fusion = (f32[8,4,32]{2,1,0:T(4,128)S(1)}, f32[8,4,32,16,32]{2,4,3,1,0:T(8,128)}) fusion(pred[4,16]{1,0:T(4,128)(4,1)S(1)} %iota_compare_fusion.2, bf16[16,32,2,8,128]{4,1,0,3,2:T(8,128)(2,1)} %all-gather.6.cloned.1.call-done, bf16[4,32,1,8,128]{4,3,2,1,0:T(8,128)(2,1)S(1)} %slice.62), kind=kOutput, calls=%fused_computation.9 | convolution fusion | flops 135789568 | bytes 3412032 | tf_op jit(solution)/shard_map/tnhd,smhd->htnsm/dot_general | solution.py:65
  459.6 6.3 %copy.33 = f32[8,4,32,512]{3,2,1,0:T(8,128)} copy(f32[8,4,32,512]{2,3,1,0:T(8,128)} %bitcast.116) | data formatting | bytes 4194304 | tf_op jit(solution)/shard_map/reshape | solution.py:68
  465.9 4.6 exponential_reduce_fusion
  470.6 0.6 fusion.20
  471.2 0.2 copy.34
  471.4 57.2 %all-gather.8.cloned.1.call-done = bf16[1024,1024]{0,1:T(8,128)(2,1)} async-done(((bf16[1024,32]{0,1:T(8,128)(2,1)}), bf16[1024,1024]{0,1:T(8,128)(2,1)}) %all-gather.8.cloned.1.call-update) | async-done | bytes 2097168 | tf_op jit(solution)/shard_map/all_gather | solution.py:145
  528.6 2.5 multiply_reduce_fusion
  531.1 1.0 convolution_convert_fusion.2
  (35 shorter events, 0.3 us)
Async XLA Ops:
  6.5 524.6 %copy-start = (bf16[1024,512]{1,0:T(8,128)(2,1)S(1)}, bf16[1024,512]{1,0:T(8,128)(2,1)}, u32[]{:S(2)}) copy-start(bf16[1024,512]{1,0:T(8,128)(2,1)} %param.17) | copy-start | bytes 3145732
  6.5 404.7 %all-gather.4.cloned.1.call-start = ((), (), s32[]{:S(2)}) async-start(), calls=%async_computation | async-start | bytes 6488064 | tf_op jit(solution)/shard_map/all_gather | solution.py:130
  7.4 11.5 %collective-permute-start = (bf16[4,1,16,128]{3,2,1,0:T(8,128)(2,1)S(1)}, bf16[4,1,16,128]{3,2,1,0:T(8,128)(2,1)S(1)}, u32[]{:S(2)}, u32[]{:S(2)}) collective-permute-start(bf16[4,1,16,128]{3,2,1,0:T(8,128)(2,1)S(1)} %get-tuple-element.7), channel_id=1, source_target_pairs={{0,4},{4,8},{8,12},{12,16},{16,20},{20,24},{24,28},{28,32},{32,36}... | collective-permute-start | bytes 49160 | tf_op jit(solution)/shard_map/ppermute | solution.py:22
  11.3 7.6 %collective-permute-start.1 = (bf16[4,1,16,128]{3,2,1,0:T(8,128)(2,1)S(1)}, bf16[4,1,16,128]{3,2,1,0:T(8,128)(2,1)S(1)}, u32[]{:S(2)}, u32[]{:S(2)}) collective-permute-start(bf16[4,1,16,128]{3,2,1,0:T(8,128)(2,1)S(1)} %get-tuple-element.8), channel_id=1, source_target_pairs={{4,0},{8,4},{12,8},{16,12},{20,16},{24,20},{28,24},{32,28},{36,32}... | collective-permute-start | bytes 49160 | tf_op jit(solution)/shard_map/ppermute | solution.py:24
  12.6 440.9 %all-gather.6.cloned.1.call-start = ((), (), s32[]{:S(2)}) async-start(), calls=%async_computation.1 | async-start | bytes 2621440 | tf_op jit(solution)/shard_map/all_gather | solution.py:135
  20.9 7.1 %copy-start.6 = (bf16[16,1,3,3,3]{0,4,3,2,1:T(4,128)(2,1)S(1)}, bf16[16,1,3,3,3]{0,4,3,2,1:T(4,128)(2,1)}, u32[]{:S(2)}) copy-start(bf16[16,1,3,3,3]{0,4,3,2,1:T(4,128)(2,1)} %param.12) | copy-start | bytes 2596
  20.9 7.1 %copy-start.7 = (pred[32,17]{0,1:T(8,128)(4,1)S(1)}, pred[32,17]{0,1:T(8,128)(4,1)}, u32[]{:S(2)}) copy-start(pred[32,17]{0,1:T(8,128)(4,1)} %constant.72) | copy-start | bytes 1636
  83.1 36.9 %collective-permute-start.2 = (bf16[4,16,1,16,128]{4,0,1,3,2:T(4,128)(2,1)}, bf16[4,16,1,16,128]{4,0,1,3,2:T(4,128)(2,1)S(1)}, u32[]{:S(2)}, u32[]{:S(2)}) collective-permute-start(bf16[4,16,1,16,128]{4,0,1,3,2:T(4,128)(2,1)} %slice_bitcast_fusion.5), channel_id=1, source_target_pairs={{0,4},{4,8},{8,12},{12,16},{16,20},{20,24},{24,28},{28,32},{32,36}... | collective-permute-start | bytes 786440 | tf_op jit(solution)/shard_map/ppermute | solution.py:22
  94.4 25.6 %collective-permute-start.3 = (bf16[4,16,1,16,128]{4,0,1,3,2:T(4,128)(2,1)S(1)}, bf16[4,16,1,16,128]{4,0,1,3,2:T(4,128)(2,1)S(1)}, u32[]{:S(2)}, u32[]{:S(2)}) collective-permute-start(bf16[4,16,1,16,128]{4,0,1,3,2:T(4,128)(2,1)S(1)} %slice_bitcast_fusion.4), channel_id=1, source_target_pairs={{4,0},{8,4},{12,8},{16,12},{20,16},{24,20},{28,24},{32,28},{36,32}... | collective-permute-start | bytes 786440 | tf_op jit(solution)/shard_map/ppermute | solution.py:24
  154.1 21.6 %copy-start.1 = (bf16[16,10,16,4,8,17]{5,4,2,3,1,0:T(8,128)(2,1)S(1)}, bf16[16,10,16,4,8,17]{5,4,2,3,1,0:T(8,128)(2,1)}, u32[]{:S(2)}) copy-start(bf16[16,10,16,4,8,17]{5,4,2,3,1,0:T(8,128)(2,1)} %reshape.265) | copy-start | bytes 8355844
  197.7 28.3 %copy-start.5 = (bf16[16,16,3,3,3]{1,0,4,3,2:T(8,128)(2,1)S(1)}, bf16[16,16,3,3,3]{1,0,4,3,2:T(8,128)(2,1)}, u32[]{:S(2)}) copy-start(bf16[16,16,3,3,3]{1,0,4,3,2:T(8,128)(2,1)} %param.13) | copy-start | bytes 41476
  372.2 27.0 %copy-start.3 = (f32[2,16,1024]{2,1,0:T(8,128)S(1)}, f32[2,16,1024]{2,1,0:T(8,128)}, u32[]{:S(2)}) copy-start(f32[2,16,1024]{2,1,0:T(8,128)} %broadcast_add_fusion) | copy-start | bytes 393220
  372.2 27.0 %copy-start.4 = (f32[4,1024]{1,0:T(4,128)S(1)}, f32[4,1024]{1,0:T(4,128)}, u32[]{:S(2)}) copy-start(f32[4,1024]{1,0:T(4,128)} %add_sine_fusion.1) | copy-start | bytes 49156
  417.4 111.2 %all-gather.8.cloned.1.call-start = ((), (), s32[]{:S(2)}) async-start(), calls=%async_computation.2 | async-start | bytes 2162688 | tf_op jit(solution)/shard_map/all_gather | solution.py:145
  465.9 4.6 copy-start.2
  465.9 4.6 slice-start
Sparse Core Ops, SparseCore 0:
  12.7 97.3 all-gather.3
  417.5 35.9 all-gather.5
  456.6 71.9 all-gather.7
where the time goes:
time: 548 us; the launch traced here: 539 us
  local copies, waits for them, and re-layouts  302 us (55%)
  waiting for transfers between devices  93 us (17%)
  matrix products  82.8 us (15%)
  other arithmetic  35.7 us (7%)
  between operations  14.3 us (3%)
  starting transfers between devices  10.9 us (2%)
    conv_general_dilated x6, local copies, waits for them, and re-layouts, convolve_strip(): lax.conv_general_dilated(field_in, kernel, (1, 1, 1), ((0, 0), (1, 1), (1...  80.3 us
    convert_element_type x8, local copies, waits for them, and re-layouts, local(): jax.nn.silu(convolve_strip(padded[:, None], conv_first))  63.9 us
    convert_element_type x4, local copies, waits for them, and re-layouts, local(): jax.nn.silu(convolve_strip(first_maps, conv_second)).astype(jnp.bfloat16)  59 us
    all_gather x1, waiting for transfers between devices, local(): lax.all_gather(mixing_weight, 'tile', axis=1, tiled=True)  57.2 us
    conv_general_dilated x2, matrix products, convolve_strip(): lax.conv_general_dilated(field_in, kernel, (1, 1, 1), ((0, 0), (1, 1), (1...  55.7 us
    transpose x1, local copies, waits for them, and re-layouts, local(): patch_cubes.transpose(0, 2, 4, 6, 1, 3, 5, 7)  51.2 us
    all_gather x1, waiting for transfers between devices, local(): keys_values = lax.all_gather(projected[:, :, 1:], 'tm', axis=0, tiled=True)  35 us
    dot_general x1, local copies, waits for them, and re-layouts, local(): jnp.dot(patch_cubes, patch_weight, preferred_element_type=jnp.float32)  27 us
  transfers between devices with their start and end apart: 7, of which 2 were waited for; matrix products, arithmetic and copies ran while one was open for 76% of the time, Pallas kernels for 0%

commit v1 on v0

--- a/solution.py
+++ b/solution.py
@@ -132,7 +132,9 @@
     ).astype(jnp.bfloat16)
     cube_count = row_count // local_frames
     projected = projected.reshape(local_frames, cube_count, 3, HEADS, HD)
-    keys_values = lax.all_gather(projected[:, :, 1:], "tm", axis=0, tiled=True)
+    x = projected[:, :, 1:]
+    sent = jnp.stack([x] * lax.axis_size("tm"))
+    keys_values = jnp.concatenate(lax.all_to_all(sent, "tm", 0, 0), axis=0)
     attended = attend_frames(
         projected[:, :, 0],
         keys_values[:, :, 0],

time: 548 us -> 496 us (0.905)
  the two profiles are of different devices: /device:TPU:0 before, /device:TPU:6 now
where the time goes in v1:
time: 496 us; the launch traced here: 487 us
  local copies, waits for them, and re-layouts  307 us (62%)
  matrix products  79.4 us (16%)
  other arithmetic  35.6 us (7%)
  waiting for transfers between devices  25.2 us (5%)
  starting transfers between devices  24.8 us (5%)
  between operations  14.6 us (3%)
    conv_general_dilated x6, local copies, waits for them, and re-layouts, convolve_strip(): lax.conv_general_dilated(field_in, kernel, (1, 1, 1), ((0, 0), (1, 1), (1...  80.3 us
    convert_element_type x8, local copies, waits for them, and re-layouts, local(): jax.nn.silu(convolve_strip(padded[:, None], conv_first))  61.9 us
    convert_element_type x4, local copies, waits for them, and re-layouts, local(): jax.nn.silu(convolve_strip(first_maps, conv_second)).astype(jnp.bfloat16)  59 us
    conv_general_dilated x2, matrix products, convolve_strip(): lax.conv_general_dilated(field_in, kernel, (1, 1, 1), ((0, 0), (1, 1), (1...  53.5 us
    transpose x1, local copies, waits for them, and re-layouts, local(): patch_cubes.transpose(0, 2, 4, 6, 1, 3, 5, 7)  51.2 us
    dot_general x1, local copies, waits for them, and re-layouts, local(): jnp.dot(patch_cubes, patch_weight, preferred_element_type=jnp.float32)  27 us
    all_to_all x1, waiting for transfers between devices, local(): keys_values = jnp.concatenate(lax.all_to_all(sent, 'tm', 0, 0), axis=0)  24.4 us
    conv_general_dilated x2, other arithmetic, convolve_strip(): lax.conv_general_dilated(field_in, kernel, (1, 1, 1), ((0, 0), (1, 1), (1...  23.9 us
  transfers between devices with their start and end apart: 7, of which 1 were waited for; matrix products, arithmetic and copies ran while one was open for 85% of the time, Pallas kernels for 0%

profile of v1, /device:TPU:6, one launch (start us, length us, event | category | flops | bytes accessed | tf_op | source)
XLA Modules:
  0.0 486.7 jit_solution(13549388040641826613)
XLA Ops:
  6.5 0.7 all-gather.3.cloned.1.call-update
  7.3 0.7 fusion.34
  8.1 3.8 collective-permute-start
  11.9 6.9 %collective-permute-start.1 = (bf16[4,1,16,128]{3,2,1,0:T(8,128)(2,1)S(1)}, bf16[4,1,16,128]{3,2,1,0:T(8,128)(2,1)S(1)}, u32[]{:S(2)}, u32[]{:S(2)}) collective-permute-start(bf16[4,1,16,128]{3,2,1,0:T(8,128)(2,1)S(1)} %get-tuple-element.8), channel_id=1, source_target_pairs={{4,0},{8,4},{12,8},{16,12},{20,16},{24,20},{28,24},{32,28},{36,32}... | collective-permute-start | bytes 49160 | tf_op jit(solution)/shard_map/ppermute | solution.py:24
  18.9 1.4 fusion.35
  20.9 0.7 add_convert_fusion.1
  21.6 0.7 add_convert_fusion
  22.3 0.7 convert_element_type.69
  22.9 0.3 add_sine_fusion
  23.2 0.2 sine_add_fusion
  23.4 0.7 broadcast_add_fusion
  24.1 0.8 add_sine_fusion.1
  24.9 0.9 maximum_bitcast_fusion.1
  25.8 0.2 pad
  26.0 0.9 reshape.262
  26.9 0.4 slice.52
  27.3 0.2 copy.79
  27.6 2.0 fusion.6
  29.6 4.4 copy.38
  34.0 17.6 %multiply_convert_fusion.1 = bf16[8,16,32,17,16]{2,4,3,1,0:T(8,128)(2,1)S(1)} fusion(pred[32,17]{0,1:T(8,128)(4,1)S(1)} %copy-done.11, bf16[1,10,16,32,19]{3,0,4,2,1:T(2,128)(2,1)S(1)} %copy.38, bf16[16,1,3,3,3]{0,4,3,2,1:T(4,128)(2,1)S(1)} %copy-done.10), kind=kOutput, calls=%fused_computation.5 | convolution fusion | flops 64339968 | bytes 2424192 | tf_op jit(solution)/shard_map/conv_general_dilated | solution.py:32
  51.6 3.4 copy-done.2
  55.0 1.8 fusion.33
  56.8 24.2 %copy.41 = bf16[8,16,32,17,16]{3,2,4,1,0:T(8,128)(2,1)} copy(bf16[8,16,32,17,16]{2,4,3,1,0:T(8,128)(2,1)} %copy-done.2) | data formatting | bytes 4456448 | tf_op jit(solution)/shard_map/convert_element_type | solution.py:95
  81.0 3.6 copy.40
  84.6 2.3 reshape.266
  86.9 1.8 slice_bitcast_fusion.5
  88.7 1.9 collective-permute-start.2
  90.6 3.6 copy.42
  94.2 2.3 reshape.268
  96.5 1.0 slice_bitcast_fusion.4
  97.6 8.5 %collective-permute-start.3 = (bf16[4,16,1,16,128]{4,0,1,3,2:T(4,128)(2,1)S(1)}, bf16[4,16,1,16,128]{4,0,1,3,2:T(4,128)(2,1)S(1)}, u32[]{:S(2)}, u32[]{:S(2)}) collective-permute-start(bf16[4,16,1,16,128]{4,0,1,3,2:T(4,128)(2,1)S(1)} %slice_bitcast_fusion.4), channel_id=1, source_target_pairs={{4,0},{8,4},{12,8},{16,12},{20,16},{24,20},{28,24},{32,28},{36,32}... | collective-permute-start | bytes 786440 | tf_op jit(solution)/shard_map/ppermute | solution.py:24
  106.0 21.6 %reshape.277 = bf16[8,16,4,136,16]{3,2,4,1,0:T(4,128)(2,1)} reshape(bf16[8,16,32,17,16]{3,2,4,1,0:T(8,128)(2,1)} %copy.41) | data formatting | bytes 4456448 | tf_op jit(solution)/shard_map/convert_element_type | solution.py:95
  127.6 2.6 slice_bitcast_fusion.1
  130.2 2.0 maximum_bitcast_fusion
  132.2 3.0 copy.61
  135.3 4.4 pad.2.clone
  139.7 24.7 %reshape.271 = bf16[16,10,16,4,8,17]{5,4,2,3,1,0:T(8,128)(2,1)} reshape(bf16[16,10,16,4,136]{4,2,3,1,0:T(8,128)(2,1)} %pad.2.clone) | data formatting | bytes 5570560 | tf_op jit(solution)/shard_map/conv_general_dilated | solution.py:32
  164.3 21.7 %slice.58 = bf16[16,10,16,4,7,2]{5,4,2,3,1,0:T(8,128)(2,1)} slice(bf16[16,10,16,4,8,17]{5,4,2,3,1,0:T(8,128)(2,1)} %reshape.271), slice={[0:16], [0:10], [0:16], [0:4], [1:8], [0:2]} | slice | bytes 573440 | tf_op jit(solution)/shard_map/conv_general_dilated | solution.py:32
  186.1 21.9 %copy_bitcast_fusion = bf16[16,10,16,32,19]{4,3,2,1,0:T(8,128)(2,1)} fusion(bf16[16,10,16,4,7,2]{5,4,2,3,1,0:T(8,128)(2,1)} %slice.58, bf16[16,10,16,4,8,17]{5,4,2,3,1,0:T(8,128)(2,1)S(1)} %copy-done.1), kind=kLoop, calls=%fused_computation.3 | loop fusion | flops 9338880 | bytes 6184960 | tf_op jit(solution)/shard_map/conv_general_dilated | solution.py:32
  208.0 28.2 %copy.45 = bf16[16,10,16,32,19]{3,0,4,2,1:T(8,128)(2,1)} copy(bf16[16,10,16,32,19]{4,3,2,1,0:T(8,128)(2,1)} %copy_bitcast_fusion) | data formatting | bytes 6225920 | tf_op jit(solution)/shard_map/conv_general_dilated | solution.py:32
  236.2 35.9 %multiply_convert_fusion = bf16[8,16,32,17,16]{2,4,3,1,0:T(8,128)(2,1)} fusion(bf16[16,10,16,32,19]{3,0,4,2,1:T(8,128)(2,1)} %copy.45, bf16[16,16,3,3,3]{1,0,4,3,2:T(8,128)(2,1)S(1)} %copy-done.9, pred[32,17]{0,1:T(8,128)(4,1)S(1)} %copy-done.11), kind=kOutput, calls=%fused_computation.4 | convolution fusion | flops 929169408 | bytes 5355552 | tf_op jit(solution)/shard_map/conv_general_dilated | solution.py:32
  272.2 24.1 %copy.46 = bf16[8,16,32,17,16]{3,2,4,1,0:T(8,128)(2,1)} copy(bf16[8,16,32,17,16]{2,4,3,1,0:T(8,128)(2,1)} %multiply_convert_fusion) | data formatting | bytes 4456448 | tf_op jit(solution)/shard_map/convert_element_type | solution.py:97
  296.3 21.3 %reshape.275 = bf16[8,16,4,136,16]{3,2,4,1,0:T(4,128)(2,1)} reshape(bf16[8,16,32,17,16]{3,2,4,1,0:T(8,128)(2,1)} %copy.46) | data formatting | bytes 4456448 | tf_op jit(solution)/shard_map/convert_element_type | solution.py:97
  317.6 2.6 slice_bitcast_fusion
  320.2 11.0 %copy.47 = bf16[4,16,8,16,128]{1,4,3,2,0:T(8,128)(2,1)} copy(bf16[4,16,8,16,128]{4,0,1,3,2:T(4,128)(2,1)S(1)} %slice_bitcast_fusion) | data formatting | bytes 4194304 | tf_op jit(solution)/shard_map/convert_element_type | solution.py:97
  331.2 51.2 %copy.48 = bf16[4,1,2,16,16,8,8,8]{3,2,7,6,5,4,0,1:T(2,128)(2,1)} copy(bf16[4,1,2,16,16,8,8,8]{4,7,3,6,2,5,0,1:T(8,128)(2,1)} %bitcast.118) | data formatting | bytes 4194304 | tf_op jit(solution)/shard_map/transpose | solution.py:109
  382.5 27.0 %dot_general.20 = bf16[4,32,8192]{1,2,0:T(8,128)(2,1)} reshape(bf16[4,1,2,16,16,8,8,8]{3,2,7,6,5,4,0,1:T(2,128)(2,1)} %copy.48) | data formatting | bytes 4194304 | tf_op jit(solution)/shard_map/dot_general | solution.py:112
  409.5 11.8 %multiply_reduce_fusion.1 = (f32[4,32]{1,0:T(4,128)S(1)}, f32[4,32,1024]{2,1,0:T(8,128)S(1)}) fusion(f32[32,1024]{1,0:T(8,128)S(1)} %bitcast.126, f32[4,1024]{1,0:T(4,128)S(1)} %copy-done.8, bf16[4,32,8192]{1,2,0:T(8,128)(2,1)} %dot_general.20, bf16[8192,1024]{1,0:T(8,128)(2,1)} %param.14), kind=kOutput, calls=%fused_computation.35 | convolution fusion | flops 2148270080 | bytes 19546624 | tf_op jit(solution)/shard_map/dot_general | solution.py:112
  421.5 5.0 %fusion.7 = bf16[16,8,24,128]{3,1,2,0:T(8,128)(2,1)S(1)} fusion(bf16[128,1024]{1,0:T(8,128)(2,1)S(1)} %fusion.22, bf16[1024,3072]{0,1:T(8,128)(2,1)} %all-gather.3.cloned.1.call-done), kind=kOutput, calls=%fused_computation.20 | convolution fusion | flops 805699584 | bytes 7340032 | tf_op jit(solution)/shard_map/dot_general | solution.py:128
  426.5 0.2 copy.62
  426.7 0.9 copy-done.5
  427.7 1.9 stack.2
  429.6 3.6 all-to-all-start
  433.5 1.0 slice.62
  434.4 24.4 %all-to-all-done = bf16[4,4,32,2,8,128]{5,2,1,4,3,0:T(8,128)(2,1)S(1)} async-done(((bf16[4,4,32,2,8,128]{5,2,1,4,3,0:T(8,128)(2,1)}), bf16[4,4,32,2,8,128]{5,2,1,4,3,0:T(8,128)(2,1)S(1)}, u32[]{:S(2)}, u32[]{:S(2)}) %all-to-all-start) | async-done | bytes 2097184 | tf_op jit(solution)/shard_map/all_to_all | solution.py:137
  458.9 0.4 copy.51
  459.3 5.0 %select_reduce_fusion = (f32[8,4,32]{2,1,0:T(4,128)S(1)}, f32[8,4,32,16,32]{2,4,3,1,0:T(8,128)}) fusion(pred[4,16]{1,0:T(4,128)(4,1)S(1)} %iota_compare_fusion.2, bf16[16,32,2,8,128]{4,1,0,3,2:T(8,128)(2,1)S(1)} %bitcast.120, bf16[4,32,1,8,128]{4,3,2,1,0:T(8,128)(2,1)S(1)} %slice.62), kind=kOutput, calls=%fused_computation.9 | convolution fusion | flops 135789568 | bytes 3412480 | tf_op jit(solution)/shard_map/tnhd,smhd->htnsm/dot_general | solution.py:65
  464.3 6.3 %copy.53 = f32[8,4,32,512]{3,2,1,0:T(8,128)} copy(f32[8,4,32,512]{2,3,1,0:T(8,128)} %bitcast.117) | data formatting | bytes 4194304 | tf_op jit(solution)/shard_map/reshape | solution.py:68
  470.6 4.5 exponential_reduce_fusion
  475.1 0.6 fusion.20
  475.8 0.2 copy.54
  476.0 0.2 copy-done.4
  476.1 2.5 multiply_reduce_fusion
  478.7 1.0 convolution_convert_fusion.2
  (43 shorter events, 0.9 us)
Async XLA Ops:
  6.5 472.1 %copy-start = (bf16[1024,512]{1,0:T(8,128)(2,1)S(1)}, bf16[1024,512]{1,0:T(8,128)(2,1)}, u32[]{:S(2)}) copy-start(bf16[1024,512]{1,0:T(8,128)(2,1)} %param.17) | copy-start | bytes 3145732
  6.5 414.9 %all-gather.3.cloned.1.call-start = ((), (), s32[]{:S(2)}) async-start(), calls=%async_computation.1 | async-start | bytes 6488064 | tf_op jit(solution)/shard_map/all_gather | solution.py:130
  7.3 468.7 %all-gather.5.cloned.1.call-start = ((), (), s32[]{:S(2)}) async-start(), calls=%async_computation.2 | async-start | bytes 2162688 | tf_op jit(solution)/shard_map/all_gather | solution.py:147
  8.1 16.8 %collective-permute-start = (bf16[4,1,16,128]{3,2,1,0:T(8,128)(2,1)S(1)}, bf16[4,1,16,128]{3,2,1,0:T(8,128)(2,1)S(1)}, u32[]{:S(2)}, u32[]{:S(2)}) collective-permute-start(bf16[4,1,16,128]{3,2,1,0:T(8,128)(2,1)S(1)} %get-tuple-element.7), channel_id=1, source_target_pairs={{0,4},{4,8},{8,12},{12,16},{16,20},{20,24},{24,28},{28,32},{32,36}... | collective-permute-start | bytes 49160 | tf_op jit(solution)/shard_map/ppermute | solution.py:22
  11.9 13.0 %collective-permute-start.1 = (bf16[4,1,16,128]{3,2,1,0:T(8,128)(2,1)S(1)}, bf16[4,1,16,128]{3,2,1,0:T(8,128)(2,1)S(1)}, u32[]{:S(2)}, u32[]{:S(2)}) collective-permute-start(bf16[4,1,16,128]{3,2,1,0:T(8,128)(2,1)S(1)} %get-tuple-element.8), channel_id=1, source_target_pairs={{4,0},{8,4},{12,8},{16,12},{20,16},{24,20},{28,24},{32,28},{36,32}... | collective-permute-start | bytes 49160 | tf_op jit(solution)/shard_map/ppermute | solution.py:24
  26.9 7.0 %copy-start.10 = (bf16[16,1,3,3,3]{0,4,3,2,1:T(4,128)(2,1)S(1)}, bf16[16,1,3,3,3]{0,4,3,2,1:T(4,128)(2,1)}, u32[]{:S(2)}) copy-start(bf16[16,1,3,3,3]{0,4,3,2,1:T(4,128)(2,1)} %param.12) | copy-start | bytes 2596
  26.9 7.0 %copy-start.11 = (pred[32,17]{0,1:T(8,128)(4,1)S(1)}, pred[32,17]{0,1:T(8,128)(4,1)}, u32[]{:S(2)}) copy-start(pred[32,17]{0,1:T(8,128)(4,1)} %constant.72) | copy-start | bytes 1636
  51.6 3.4 copy-start.2
  88.7 41.5 %collective-permute-start.2 = (bf16[4,16,1,16,128]{4,0,1,3,2:T(4,128)(2,1)}, bf16[4,16,1,16,128]{4,0,1,3,2:T(4,128)(2,1)S(1)}, u32[]{:S(2)}, u32[]{:S(2)}) collective-permute-start(bf16[4,16,1,16,128]{4,0,1,3,2:T(4,128)(2,1)} %slice_bitcast_fusion.5), channel_id=1, source_target_pairs={{0,4},{4,8},{8,12},{12,16},{16,20},{20,24},{24,28},{28,32},{32,36}... | collective-permute-start | bytes 786440 | tf_op jit(solution)/shard_map/ppermute | solution.py:22
  97.6 32.6 %collective-permute-start.3 = (bf16[4,16,1,16,128]{4,0,1,3,2:T(4,128)(2,1)S(1)}, bf16[4,16,1,16,128]{4,0,1,3,2:T(4,128)(2,1)S(1)}, u32[]{:S(2)}, u32[]{:S(2)}) collective-permute-start(bf16[4,16,1,16,128]{4,0,1,3,2:T(4,128)(2,1)S(1)} %slice_bitcast_fusion.4), channel_id=1, source_target_pairs={{4,0},{8,4},{12,8},{16,12},{20,16},{24,20},{28,24},{32,28},{36,32}... | collective-permute-start | bytes 786440 | tf_op jit(solution)/shard_map/ppermute | solution.py:24
  164.3 21.7 %copy-start.1 = (bf16[16,10,16,4,8,17]{5,4,2,3,1,0:T(8,128)(2,1)S(1)}, bf16[16,10,16,4,8,17]{5,4,2,3,1,0:T(8,128)(2,1)}, u32[]{:S(2)}) copy-start(bf16[16,10,16,4,8,17]{5,4,2,3,1,0:T(8,128)(2,1)} %reshape.271) | copy-start | bytes 8355844
  208.0 28.3 %copy-start.9 = (bf16[16,16,3,3,3]{1,0,4,3,2:T(8,128)(2,1)S(1)}, bf16[16,16,3,3,3]{1,0,4,3,2:T(8,128)(2,1)}, u32[]{:S(2)}) copy-start(bf16[16,16,3,3,3]{1,0,4,3,2:T(8,128)(2,1)} %param.13) | copy-start | bytes 41476
  382.4 27.0 %copy-start.7 = (f32[2,16,1024]{2,1,0:T(8,128)S(1)}, f32[2,16,1024]{2,1,0:T(8,128)}, u32[]{:S(2)}) copy-start(f32[2,16,1024]{2,1,0:T(8,128)} %broadcast_add_fusion) | copy-start | bytes 393220
  382.4 27.0 %copy-start.8 = (f32[4,1024]{1,0:T(4,128)S(1)}, f32[4,1024]{1,0:T(4,128)}, u32[]{:S(2)}) copy-start(f32[4,1024]{1,0:T(4,128)} %add_sine_fusion.1) | copy-start | bytes 49156
  421.3 8.3 %copy-start.3 = (f32[4,32,1024]{2,1,0:T(8,128)}, f32[4,32,1024]{2,1,0:T(8,128)S(1)}, u32[]{:S(2)}) copy-start(f32[4,32,1024]{2,1,0:T(8,128)S(1)} %get-tuple-element.13) | copy-start | bytes 1572868
  426.7 0.9 copy-start.5
  429.6 29.3 %all-to-all-start = ((bf16[4,4,32,2,8,128]{5,2,1,4,3,0:T(8,128)(2,1)}), bf16[4,4,32,2,8,128]{5,2,1,4,3,0:T(8,128)(2,1)S(1)}, u32[]{:S(2)}, u32[]{:S(2)}) async-start(bf16[4,4,32,2,8,128]{5,2,1,4,3,0:T(8,128)(2,1)} %stack.2), calls=%async_computation | async-start | bytes 4194304 | tf_op jit(solution)/shard_map/all_to_all | solution.py:137
  470.6 4.6 copy-start.6
  475.1 1.0 copy-start.4
Sparse Core Ops, SparseCore 0:
  10.4 98.9 all-gather.2
  112.5 65.5 all-gather.4
